TPU v7x, 32 devices: a whole 2x2x4 slice. The times are simulated.
32 devices in a mesh: grp: 2 (over x), tile: 8 (over z, y), freq: 2 (over core).
Axes of the slice: x: 2, y: 2, z: 4, core: 2. Of those that a mesh axis runs over, the one named last changes fastest.
Arguments:
- green_recv: bfloat16 [4, 2, 1024, 4096], P(('grp', 'freq'), None, None, 'tile'), parts along dimension 0, may hold values from -2 to 2
- green_shot: bfloat16 [4, 2, 512, 4096], P(('grp', 'freq'), None, None, 'tile'), parts along dimension 0, may hold values from -2.5 to 2.5
- band_mask: int32 [16, 5], P('grp'), parts along dimension 0, may hold values from 0 to 1, as said below
- live_counts: int32 [16], P('grp'), parts along dimension 0, may hold values from 128 to 512, as said below
- freq_bins: int32 [4], P(('grp', 'freq')), parts along dimension 0, may hold values from 256 to 511
Outputs:
- hessian: float32 [8192, 5, 512], P(('grp', 'tile', 'freq')), parts along dimension 0
There are 2 independent parts, one for each index of `grp`. A program takes and returns all parts, laid end to end along the dimension named above; each array names one. Nothing has to cross between parts.
Inputs may be any that keep to these rules, and one draw needn't show every extreme that they name: band_mask[t, 2 + d] equals band_mask[t + d, 2 - d], is 1 at d = 0, is 0 where t + d lies outside the tiles, and some tile has all 5 slots at 1. `live_counts`: some tile has all 512 points live.
All inputs are finite; a program needn't handle non-finite values.
Results may differ from a plain program's by a relative error of at most 0.00065.
Values may be sent and summed in bfloat16 or wider, within the bound.
A program may use at most 64 MiB of HBM per device.

v0:
```python
import functools

import jax
import jax.numpy as jnp
from jax import lax
from jax.experimental import pallas as pl
from jax.experimental.pallas import tpu as pltpu
from jax.sharding import PartitionSpec as P

BINS = 512
VMEM_MIB = 60
MESH = pl.DeviceIdType.MESH
PAIR = {(1, 0): 0, (2, 0): 1, (2, 1): 2, (1, 2): 2}
ROW = {1: 0, 2: 1, -1: 2, -2: 3}


def place(tiles):
    t = lax.axis_index("tile")
    f = lax.axis_index("freq")
    step = 1 - 2 * f
    r = f * (tiles - 1) + step * t
    return t, f, step, r, lax.rem(r, 2) == 0


def band_kernel(tiles, recv_ref, shot_ref, bins_ref, inbox, kept,
                far_r, far_s, left_r, left_s, own, self_out, self_in, outbox, turned,
                own_sem, kept_sem, data_send, data_recv, res_send, res_recv, self_send, self_recv):
    t, f, step, r, heavy = place(tiles)
    depth_r, points = recv_ref.shape
    depth_s = shot_ref.shape[0]
    half = points // 2
    part = half // 2
    has_far = r + 2 < tiles
    weight_root = bins_ref[0].astype(jnp.float32) / BINS
    weight = (weight_root * weight_root) * (weight_root * weight_root)

    def columns(j):
        return pl.ds(pl.multiple_of(j * half, half), half)

    def parts(i):
        return pl.ds(pl.multiple_of(i * part, part), part)

    def own_copy(which, j):
        src, dst = ((recv_ref, far_r), (shot_ref, far_s))[which]
        return pltpu.make_async_copy(src.at[:, columns(j)], dst.at[0, j], own_sem.at[which, j])

    def data_copy(which, i, distance):
        src, dst = ((recv_ref, far_r), (shot_ref, far_s))[which]
        return pltpu.make_async_remote_copy(
            src_ref=src.at[:, parts(i)], dst_ref=dst.at[distance, i // 2, :, parts(i % 2)],
            send_sem=data_send.at[which, i, distance - 1], recv_sem=data_recv.at[which, i, distance - 1],
            device_id={"tile": t - step * distance}, device_id_type=MESH)

    barrier = pltpu.get_barrier_semaphore()
    for distance in range(-2, 3):
        near = t + distance
        for turn in range(2):
            if distance == 0 and turn == 0:
                continue
            other = f if turn == 0 else 1 - f

            @pl.when((near >= 0) & (near < tiles))
            def _():
                pl.semaphore_signal(barrier, inc=1, device_id={"tile": near, "freq": other}, device_id_type=MESH)
    reached = jnp.minimum(t, 2) + jnp.minimum(tiles - 1 - t, 2)
    for j in range(2):
        for which in range(2):
            own_copy(which, j).start()

    pl.semaphore_wait(barrier, 2 * reached + 1)

    for i in range(4):
        for which in range(2):
            @pl.when(jnp.logical_not(heavy))
            def _():
                data_copy(which, i, 1).start()

            @pl.when(r >= 2)
            def _():
                data_copy(which, i, 2).start()

    def build_left(slot, i):
        for src, dst, depth in ((far_r, left_r, depth_r // 2), (far_s, left_s, depth_s // 2)):
            re = src[slot, i // 2, 0:depth, parts(i % 2)].T
            im = src[slot, i // 2, depth:2 * depth, parts(i % 2)].T
            dst[slot, i, 0:part, 0:depth] = re
            dst[slot, i, 0:part, depth:2 * depth] = im
            dst[slot, i, part:half, 0:depth] = im
            dst[slot, i, part:half, depth:2 * depth] = -re

    def block(left, i, right, h):
        rr = jnp.dot(left_r[left, i], far_r[right, h], preferred_element_type=jnp.float32)
        ss = jnp.dot(left_s[left, i], far_s[right, h], preferred_element_type=jnp.float32)
        return (rr[:part] * ss[:part] - rr[part:] * ss[part:]) * weight

    def origin_at(h):
        return jnp.where(h == f, 0, 1)

    def plain_send(left, i, right, h, n):
        k, origin, row = PAIR[left, right], origin_at(i // 2), ROW[right - left]
        return pltpu.make_async_remote_copy(
            src_ref=outbox.at[k, n], dst_ref=inbox.at[origin, row, parts(i % 2), columns(h)],
            send_sem=res_send.at[k, 0], recv_sem=res_recv.at[origin, row],
            device_id={"tile": t + step * left, "freq": i // 2}, device_id_type=MESH)

    def turned_send(left, i, right, h, n):
        k, origin, row = PAIR[left, right], origin_at(h), ROW[left - right]
        return pltpu.make_async_remote_copy(
            src_ref=turned.at[k, n], dst_ref=inbox.at[origin, row, :, parts(i)],
            send_sem=res_send.at[k, 1], recv_sem=res_recv.at[origin, row],
            device_id={"tile": t + step * right, "freq": h}, device_id_type=MESH)

    def unit(left, i, right, h, n):
        k = PAIR[left, right]
        value = block(left, i, right, h)
        outbox[k, n] = value.astype(jnp.bfloat16)
        plain_send(left, i, right, h, n).start()
        if right == 0:
            @pl.when(h == f)
            def _():
                own[left, :, parts(i)] = value.T

            @pl.when(h != f)
            def _():
                turned[k, n] = value.T.astype(jnp.bfloat16)
                turned_send(left, i, right, h, n).start()
        else:
            turned[k, n] = value.T.astype(jnp.bfloat16)
            turned_send(left, i, right, h, n).start()

    def self_copy():
        return pltpu.make_async_remote_copy(
            src_ref=self_out, dst_ref=self_in, send_sem=self_send, recv_sem=self_recv,
            device_id={"freq": 1 - f}, device_id_type=MESH)

    for j in range(2):
        for which in range(2):
            own_copy(which, j).wait()

    @pl.loop(0, 4)
    def _(i):
        build_left(0, i)

    for target, dest in ((1 - f, self_out), (f, own.at[0])):
        @pl.loop(0, 4)
        def _(m):
            dest[parts(m // 2), columns(m % 2)] = block(0, 2 * target + m // 2, 0, m % 2)

        if dest is self_out:
            self_copy().start()

    @pl.loop(0, 4)
    def _(i):
        @pl.when(heavy)
        def _():
            for which in range(2):
                data_copy(which, i, 1).wait_recv()
            build_left(1, i)

            @pl.loop(0, 2)
            def _(h):
                unit(1, i, 0, h, 2 * i + h)

        @pl.when(heavy & has_far & (i >= 2))
        def _():
            unit(1, i, 2, 0, 2 * i - 3)

        @pl.when(has_far)
        def _():
            for which in range(2):
                data_copy(which, i, 2).wait_recv()
            build_left(2, i)

            @pl.loop(0, 2)
            def _(h):
                unit(2, i, 0, h, 2 * i + h)

        @pl.when(heavy & has_far)
        def _():
            @pl.loop(0, jnp.where(i == 1, 2, jnp.where(i == 0, 0, 2 * i - 3)))
            def _(m):
                n = jnp.where(i == 1, 2 * m, i + 2 + m)
                unit(2, n // 2, 1, n % 2, n)

    self_copy().wait_recv()
    own[0] = own[0] + self_in[...]
    keep_copy = pltpu.make_async_copy(own, kept, kept_sem)
    keep_copy.start()

    def wait_inbox(origin, row):
        pltpu.make_async_remote_copy(
            src_ref=inbox.at[origin, row], dst_ref=inbox.at[origin, row],
            send_sem=res_send.at[0, 0], recv_sem=res_recv.at[origin, row],
            device_id={"freq": 1 - f}, device_id_type=MESH).wait_recv()

    for delta, row in ROW.items():
        @pl.when((r + delta >= 0) & (r + delta < tiles))
        def _():
            wait_inbox(1, ROW[-delta])
            if delta == 1:
                pl.when(jnp.logical_not(heavy))(lambda: wait_inbox(0, row))
            elif delta < 0:
                wait_inbox(0, row)

    keep_copy.wait()
    self_copy().wait_send()
    for i in range(4):
        for which in range(2):
            @pl.when(jnp.logical_not(heavy))
            def _():
                data_copy(which, i, 1).wait_send()

            @pl.when(r >= 2)
            def _():
                data_copy(which, i, 2).wait_send()

    def wait_sent(box, sem):
        pltpu.make_async_remote_copy(
            src_ref=box, dst_ref=box, send_sem=sem, recv_sem=res_recv.at[0, 0],
            device_id={"freq": 1 - f}, device_id_type=MESH).wait_send()

    for k, made in enumerate((heavy, has_far, heavy & has_far)):
        @pl.when(made)
        def _():
            wait_sent(outbox.at[k], res_send.at[k, 0])
            wait_sent(turned.at[k] if k == 2 else turned.at[k, 0:4], res_send.at[k, 1])


def join_kernel(tiles, radius, inbox_ref, kept_ref, band_ref, live_ref, out_ref, inbox, kept, out, inbox_sem, kept_sem, out_sem):
    t, f, step, r, heavy = place(tiles)
    _, half, points = kept.shape

    def inbox_copy(origin, row):
        return pltpu.make_async_copy(inbox_ref.at[origin, row], inbox.at[origin, row], inbox_sem.at[origin, row])

    def kept_copy(k):
        return pltpu.make_async_copy(kept_ref.at[k], kept.at[k], kept_sem.at[k])

    def out_copy(slot):
        return pltpu.make_async_copy(out.at[slot], out_ref.at[slot], out_sem.at[slot])

    order = (0, 2, 1, -1, -2)
    for delta in order:
        if delta == 1:
            pl.when(heavy)(kept_copy(1).start)
            pl.when(jnp.logical_not(heavy))(inbox_copy(0, ROW[1]).start)
        elif delta >= 0:
            kept_copy(delta).start()
        else:
            inbox_copy(0, ROW[delta]).start()
        if delta != 0:
            inbox_copy(1, ROW[-delta]).start()
    rows = lax.broadcasted_iota(jnp.int32, (half, points), 0) + f * half
    cols = lax.broadcasted_iota(jnp.int32, (half, points), 1)
    row_live = rows < live_ref[t]
    for delta in order:
        near = t + step * delta
        slot = radius + step * delta
        exists = (r + delta >= 0) & (r + delta < tiles)
        if delta == 1:
            pl.when(heavy)(kept_copy(1).wait)
            pl.when(jnp.logical_not(heavy))(inbox_copy(0, ROW[1]).wait)
        elif delta >= 0:
            kept_copy(delta).wait()
        else:
            inbox_copy(0, ROW[delta]).wait()
        if delta != 0:
            inbox_copy(1, ROW[-delta]).wait()

        def emit(read, near=near, slot=slot):
            keep = row_live & (cols < live_ref[near]) & (band_ref[t, slot] > 0)
            out[slot] = jnp.where(keep, read(), 0.0)

        def kept_sum(delta=delta):
            if delta == 0:
                return kept[0]
            return kept[delta] + inbox[1, ROW[-delta]].astype(jnp.float32)

        def inbox_sum(delta=delta):
            return inbox[0, ROW[delta]].astype(jnp.float32) + inbox[1, ROW[-delta]].astype(jnp.float32)

        if delta in (0, 2):
            pl.when(exists)(functools.partial(emit, kept_sum))
        elif delta == 1:
            pl.when(exists & heavy)(functools.partial(emit, kept_sum))
            pl.when(exists & jnp.logical_not(heavy))(functools.partial(emit, inbox_sum))
        else:
            pl.when(exists)(functools.partial(emit, inbox_sum))

        @pl.when(jnp.logical_not(exists))
        def _():
            out[slot] = jnp.zeros((half, points), jnp.float32)

        out_copy(slot).start()
    for slot in range(2 * radius + 1):
        out_copy(slot).wait()


def per_device(green_recv, green_shot, band_mask, live_counts, freq_bins):
    tiles = lax.axis_size("tile")
    points = green_recv.shape[3]
    slots = band_mask.shape[1]
    half = points // 2
    depth_r = 2 * green_recv.shape[2]
    depth_s = 2 * green_shot.shape[2]
    bf16, f32 = jnp.bfloat16, jnp.float32
    dma = pltpu.SemaphoreType.DMA
    smem = pl.BlockSpec(memory_space=pltpu.SMEM)
    anywhere = pl.BlockSpec(memory_space=pl.ANY)
    inbox, kept = pl.pallas_call(
        functools.partial(band_kernel, tiles),
        out_shape=(
            jax.ShapeDtypeStruct((2, 4, half, points), bf16),
            jax.ShapeDtypeStruct((3, half, points), f32),
        ),
        in_specs=[anywhere, anywhere, smem],
        out_specs=(anywhere, anywhere),
        scratch_shapes=[
            pltpu.VMEM((3, 2, depth_r, half), bf16),
            pltpu.VMEM((3, 2, depth_s, half), bf16),
            pltpu.VMEM((3, 4, half, depth_r), bf16),
            pltpu.VMEM((3, 4, half, depth_s), bf16),
            pltpu.VMEM((3, half, points), f32),
            pltpu.VMEM((half, points), f32),
            pltpu.VMEM((half, points), f32),
            pltpu.VMEM((3, 8, half // 2, half), bf16),
            pltpu.VMEM((3, 8, half, half // 2), bf16),
            dma((2, 2)),
            dma,
            dma((2, 4, 2)),
            dma((2, 4, 2)),
            dma((3, 2)),
            dma((2, 4)),
            dma,
            dma,
        ],
        compiler_params=pltpu.CompilerParams(
            collective_id=0, has_side_effects=True, vmem_limit_bytes=VMEM_MIB * 1024 * 1024),
    )(green_recv.reshape(depth_r, points), green_shot.reshape(depth_s, points), freq_bins)
    band = pl.pallas_call(
        functools.partial(join_kernel, tiles, slots // 2),
        out_shape=jax.ShapeDtypeStruct((slots, half, points), f32),
        in_specs=[anywhere, anywhere, smem, smem],
        out_specs=anywhere,
        scratch_shapes=[
            pltpu.VMEM((2, 4, half, points), bf16),
            pltpu.VMEM((3, half, points), f32),
            pltpu.VMEM((slots, half, points), f32),
            dma((2, 4)),
            dma((3,)),
            dma((slots,)),
        ],
        compiler_params=pltpu.CompilerParams(vmem_limit_bytes=VMEM_MIB * 1024 * 1024),
    )(inbox, kept, band_mask, live_counts)
    return jnp.transpose(band, (1, 0, 2))


def solution(mesh):
    return jax.shard_map(
        per_device,
        mesh=mesh,
        in_specs=(
            P(("grp", "freq"), None, None, "tile"),
            P(("grp", "freq"), None, None, "tile"),
            P("grp", None),
            P("grp"),
            P(("grp", "freq")),
        ),
        out_specs=P(("grp", "tile", "freq"), None, None),
        check_vma=False,
    )
```

profile of v0, /device:TPU:13, one launch (start us, length us, event | category | flops | bytes accessed | tf_op | source)
XLA Modules:
  0.0 59.4 jit_solution(10419763902278982355)
XLA Ops:
  0.7 54.9 %shard_map.55 = (bf16[2,4,256,512]{3,2,1,0:T(8,128)(2,1)}, f32[3,256,512]{2,1,0:T(8,128)}) custom-call(bf16[2048,512]{1,0:T(8,128)(2,1)} %bitcast.3, bf16[1024,512]{1,0:T(8,128)(2,1)} %bitcast.4, s32[1]{0:T(128)S(6)} %copy.6.bins_ref), custom_call_target="tpu_custom_call" | custom-call | tf_op jit(solution)/shard_map/pallas_call | solution.py:310
  55.5 3.9 %shard_map.56 = f32[5,256,512]{2,1,0:T(8,128)} custom-call(bf16[2,4,256,512]{3,2,1,0:T(8,128)(2,1)} %get-tuple-element.7.inbox_ref, f32[3,256,512]{2,1,0:T(8,128)} %get-tuple-element.8.kept_ref, s32[8,5]{1,0:T(8,128)} %band_ref.1, s32[8]{0:T(128)} %live_ref.1), custom_call_target="tpu_custom_call" | custom-call | tf_op jit(solution)/shard_map/pallas_call | solution.py:340
where the time goes:
time: 59.6 us; the launch traced here: 59.4 us
  Pallas kernels  58.8 us (99%)
  between operations  0.66 us (1%)
    pallas_call x1, Pallas kernels, per_device(): pl.pallas_call(functools.partial(band_kernel, tiles), out_shape=(jax.Shap...  54.9 us
    pallas_call x1, Pallas kernels, per_device(): pl.pallas_call(functools.partial(join_kernel, tiles, slots // 2), out_sha...  3.87 us

commit v1 on v0

v1 whole, which is shorter than its diff:
```python
import functools

import jax
import jax.numpy as jnp
from jax import lax
from jax.experimental import pallas as pl
from jax.experimental.pallas import tpu as pltpu
from jax.sharding import PartitionSpec as P

BINS = 512
VMEM_MIB = 44
MESH = pl.DeviceIdType.MESH
PAIR = {(1, 0): 0, (2, 0): 1, (2, 1): 2, (1, 2): 2}
ROW = {1: 0, 2: 1, -1: 2, -2: 3}


def place(tiles):
    t = lax.axis_index("tile")
    f = lax.axis_index("freq")
    step = 1 - 2 * f
    r = f * (tiles - 1) + step * t
    return t, f, step, r, lax.rem(r, 2) == 0


def band_kernel(tiles, radius, recv_ref, shot_ref, bins_ref, band_hbm, live_hbm, out,
                band_ref, live_ref, table_sem, inbox, far_r, far_s, left_r, left_s, own, self_out, self_in, outbox, turned,
                own_sem, data_send, data_recv, res_send, res_recv, self_send, self_recv):
    t, f, step, r, heavy = place(tiles)
    depth_r, points = recv_ref.shape
    depth_s = shot_ref.shape[0]
    half = points // 2
    part = half // 2
    has_far = r + 2 < tiles
    tables = [pltpu.make_async_copy(src, dst, table_sem.at[k]) for k, (src, dst) in enumerate(
        ((band_hbm, band_ref), (live_hbm, live_ref)))]
    for table in tables:
        table.start()

    def columns(j):
        return pl.ds(pl.multiple_of(j * half, half), half)

    def parts(i):
        return pl.ds(pl.multiple_of(i * part, part), part)

    def own_copy(which, j):
        src, dst = ((recv_ref, far_r), (shot_ref, far_s))[which]
        return pltpu.make_async_copy(src.at[:, columns(j)], dst.at[0, j], own_sem.at[which, j])

    def data_copy(which, i, distance):
        src, dst = ((recv_ref, far_r), (shot_ref, far_s))[which]
        return pltpu.make_async_remote_copy(
            src_ref=src.at[:, parts(i)], dst_ref=dst.at[distance, i // 2, :, parts(i % 2)],
            send_sem=data_send.at[which, i, distance - 1], recv_sem=data_recv.at[which, i, distance - 1],
            device_id={"tile": t - step * distance}, device_id_type=MESH)

    barrier = pltpu.get_barrier_semaphore()
    for distance in range(-2, 3):
        near = t + distance
        for turn in range(2):
            if distance == 0 and turn == 0:
                continue
            other = f if turn == 0 else 1 - f

            @pl.when((near >= 0) & (near < tiles))
            def _():
                pl.semaphore_signal(barrier, inc=1, device_id={"tile": near, "freq": other}, device_id_type=MESH)
    reached = jnp.minimum(t, 2) + jnp.minimum(tiles - 1 - t, 2)
    for j in range(2):
        for which in range(2):
            own_copy(which, j).start()

    pl.semaphore_wait(barrier, 2 * reached + 1)

    for i in range(4):
        for which in range(2):
            @pl.when(jnp.logical_not(heavy))
            def _():
                data_copy(which, i, 1).start()

            @pl.when(r >= 2)
            def _():
                data_copy(which, i, 2).start()

    def build_left(slot, i):
        for src, dst, depth in ((far_r, left_r, depth_r // 2), (far_s, left_s, depth_s // 2)):
            re = src[slot, i // 2, 0:depth, parts(i % 2)].T
            im = src[slot, i // 2, depth:2 * depth, parts(i % 2)].T
            dst[slot, i, 0:part, 0:depth] = re
            dst[slot, i, 0:part, depth:2 * depth] = im
            dst[slot, i, part:half, 0:depth] = im
            dst[slot, i, part:half, depth:2 * depth] = -re

    def block(left, i, right, h):
        rr = jnp.dot(left_r[left, i], far_r[right, h], preferred_element_type=jnp.float32)
        ss = jnp.dot(left_s[left, i], far_s[right, h], preferred_element_type=jnp.float32)
        return (rr[:part] * ss[:part] - rr[part:] * ss[part:]) * weight

    def origin_at(h):
        return jnp.where(h == f, 0, 1)

    def plain_send(left, i, right, h, n):
        k, origin, row = PAIR[left, right], origin_at(i // 2), ROW[right - left]
        return pltpu.make_async_remote_copy(
            src_ref=outbox.at[k, n], dst_ref=inbox.at[origin, row, parts(i % 2), columns(h)],
            send_sem=res_send.at[k, 0], recv_sem=res_recv.at[origin, row],
            device_id={"tile": t + step * left, "freq": i // 2}, device_id_type=MESH)

    def turned_send(left, i, right, h, n):
        k, origin, row = PAIR[left, right], origin_at(h), ROW[left - right]
        return pltpu.make_async_remote_copy(
            src_ref=turned.at[k, n], dst_ref=inbox.at[origin, row, :, parts(i)],
            send_sem=res_send.at[k, 1], recv_sem=res_recv.at[origin, row],
            device_id={"tile": t + step * right, "freq": h}, device_id_type=MESH)

    def unit(left, i, right, h, n, send):
        k = PAIR[left, right]
        value = block(left, i, right, h)
        outbox[k, n] = value.astype(jnp.bfloat16)
        if send:
            plain_send(left, i, right, h, n).start()
        if right == 0:
            @pl.when(h == f)
            def _():
                own[left, :, parts(i)] = value.T

            @pl.when(h != f)
            def _():
                turned[k, n] = value.T.astype(jnp.bfloat16)
                turned_send(left, i, right, h, n).start()
        else:
            turned[k, n] = value.T.astype(jnp.bfloat16)
            if send:
                turned_send(left, i, right, h, n).start()

    def self_copy():
        return pltpu.make_async_remote_copy(
            src_ref=self_out, dst_ref=self_in, send_sem=self_send, recv_sem=self_recv,
            device_id={"freq": 1 - f}, device_id_type=MESH)

    for j in range(2):
        for which in range(2):
            own_copy(which, j).wait()

    @pl.loop(0, 4)
    def _(i):
        build_left(0, i)

    for table in tables:
        table.wait()
    weight_root = bins_ref[0].astype(jnp.float32) / BINS
    weight = (weight_root * weight_root) * (weight_root * weight_root)

    for target, dest in ((1 - f, self_out), (f, own.at[0])):
        @pl.loop(0, 4)
        def _(m):
            dest[parts(m // 2), columns(m % 2)] = block(0, 2 * target + m // 2, 0, m % 2)

        if dest is self_out:
            self_copy().start()

    def mixed(first, bound, send):
        @pl.loop(first, bound)
        def _(n):
            unit(2, n // 2, 1, n % 2, n, send)

    @pl.loop(0, 3)
    def _(i):
        @pl.when(heavy)
        def _():
            for which in range(2):
                data_copy(which, i, 1).wait_recv()
            build_left(1, i)

            @pl.loop(0, 2)
            def _(h):
                unit(1, i, 0, h, 2 * i + h, False)

        @pl.when(heavy & has_far & (i == 2))
        def _():
            unit(1, i, 2, 0, 1, False)

        @pl.when(has_far)
        def _():
            for which in range(2):
                data_copy(which, i, 2).wait_recv()
            build_left(2, i)

            @pl.loop(0, 2)
            def _(h):
                unit(2, i, 0, h, 2 * i + h, False)

        @pl.when(heavy & has_far)
        def _():
            @pl.loop(0, jnp.where(i == 1, 2, jnp.where(i == 0, 0, 1)))
            def _(m):
                n = jnp.where(i == 1, 2 * m, 4)
                unit(2, n // 2, 1, n % 2, n, False)

    @pl.when(heavy)
    def _():
        for which in range(2):
            data_copy(which, 3, 1).wait_recv()

        @pl.loop(0, 6)
        def _(n):
            plain_send(1, n // 2, 0, n % 2, n).start()

        @pl.when(has_far)
        def _():
            plain_send(1, 2, 2, 0, 1).start()

            @pl.loop(0, 3)
            def _(m):
                turned_send(2, m, 1, 0, 2 * m).start()

        build_left(1, 3)

        @pl.loop(0, 2)
        def _(h):
            unit(1, 3, 0, h, 6 + h, True)

    @pl.when(has_far)
    def _():
        for which in range(2):
            data_copy(which, 3, 2).wait_recv()

        @pl.loop(0, 6)
        def _(n):
            plain_send(2, n // 2, 0, n % 2, n).start()

        @pl.when(heavy)
        def _():
            turned_send(1, 2, 2, 0, 1).start()

            @pl.loop(0, 3)
            def _(m):
                plain_send(2, m, 1, 0, 2 * m).start()

            unit(1, 3, 2, 0, 3, True)

        build_left(2, 3)

        @pl.loop(0, 2)
        def _(h):
            unit(2, 3, 0, h, 6 + h, True)

        @pl.when(heavy)
        def _():
            @pl.loop(5, 8)
            def _(n):
                unit(2, n // 2, 1, n % 2, n, True)

    rows = lax.broadcasted_iota(jnp.int32, (half, points), 0) + f * half
    cols = lax.broadcasted_iota(jnp.int32, (half, points), 1)
    row_live = rows < live_ref[t]

    def wait_inbox(origin, row):
        pltpu.make_async_remote_copy(
            src_ref=inbox.at[origin, row], dst_ref=inbox.at[origin, row],
            send_sem=res_send.at[0, 0], recv_sem=res_recv.at[origin, row],
            device_id={"freq": 1 - f}, device_id_type=MESH).wait_recv()

    def emit(delta, value):
        near, slot = t + step * delta, radius + step * delta
        keep = row_live & (cols < live_ref[near]) & (band_ref[t, slot] > 0)
        out[slot] = jnp.where(keep, value, 0.0)

    self_copy().wait_recv()
    emit(0, own[0] + self_in[...])
    for delta in ROW:
        exists = (r + delta >= 0) & (r + delta < tiles)

        @pl.when(jnp.logical_not(exists))
        def _():
            out[radius + step * delta] = jnp.zeros((half, points), jnp.float32)

    for delta in (2, -2, 1, -1):
        row = ROW[delta]
        exists = (r + delta >= 0) & (r + delta < tiles)

        def own_sum():
            wait_inbox(1, ROW[-delta])
            emit(delta, own[delta] + inbox[1, ROW[-delta]].astype(jnp.float32))

        def inbox_sum():
            wait_inbox(0, row)
            wait_inbox(1, ROW[-delta])
            emit(delta, inbox[0, row].astype(jnp.float32) + inbox[1, ROW[-delta]].astype(jnp.float32))

        if delta == 2:
            pl.when(exists)(own_sum)
        elif delta == 1:
            pl.when(exists & heavy)(own_sum)
            pl.when(exists & jnp.logical_not(heavy))(inbox_sum)
        else:
            pl.when(exists)(inbox_sum)

    self_copy().wait_send()
    for i in range(4):
        for which in range(2):
            @pl.when(jnp.logical_not(heavy))
            def _():
                data_copy(which, i, 1).wait_send()

            @pl.when(r >= 2)
            def _():
                data_copy(which, i, 2).wait_send()

    def wait_sent(box, sem):
        pltpu.make_async_remote_copy(
            src_ref=box, dst_ref=box, send_sem=sem, recv_sem=res_recv.at[0, 0],
            device_id={"freq": 1 - f}, device_id_type=MESH).wait_send()

    for k, made in enumerate((heavy, has_far, heavy & has_far)):
        @pl.when(made)
        def _():
            wait_sent(outbox.at[k], res_send.at[k, 0])
            wait_sent(turned.at[k] if k == 2 else turned.at[k, 0:4], res_send.at[k, 1])


def store_kernel(band, out_ref, out_sem):
    slots = band.shape[0]
    for slot in range(slots):
        pltpu.make_async_copy(band.at[slot], out_ref.at[slot], out_sem.at[slot]).start()
    for slot in range(slots):
        pltpu.make_async_copy(band.at[slot], out_ref.at[slot], out_sem.at[slot]).wait()


def in_hbm(array):
    return pltpu.with_memory_space_constraint(array, pltpu.HBM)


def per_device(green_recv, green_shot, band_mask, live_counts, freq_bins):
    tiles = lax.axis_size("tile")
    points = green_recv.shape[3]
    slots = band_mask.shape[1]
    half = points // 2
    depth_r = 2 * green_recv.shape[2]
    depth_s = 2 * green_shot.shape[2]
    bf16, f32 = jnp.bfloat16, jnp.float32
    dma = pltpu.SemaphoreType.DMA
    anywhere = pl.BlockSpec(memory_space=pltpu.HBM)
    band = pl.pallas_call(
        functools.partial(band_kernel, tiles, slots // 2),
        out_shape=jax.ShapeDtypeStruct((slots, half, points), f32),
        in_specs=[anywhere, anywhere, pl.BlockSpec(memory_space=pltpu.SMEM), anywhere, anywhere],
        out_specs=pl.BlockSpec(memory_space=pltpu.VMEM),
        scratch_shapes=[
            pltpu.SMEM(band_mask.shape, jnp.int32),
            pltpu.SMEM(live_counts.shape, jnp.int32),
            dma((2,)),
            pltpu.VMEM((2, 4, half, points), bf16),
            pltpu.VMEM((3, 2, depth_r, half), bf16),
            pltpu.VMEM((3, 2, depth_s, half), bf16),
            pltpu.VMEM((3, 4, half, depth_r), bf16),
            pltpu.VMEM((3, 4, half, depth_s), bf16),
            pltpu.VMEM((3, half, points), f32),
            pltpu.VMEM((half, points), f32),
            pltpu.VMEM((half, points), f32),
            pltpu.VMEM((3, 8, half // 2, half), bf16),
            pltpu.VMEM((3, 8, half, half // 2), bf16),
            dma((2, 2)),
            dma((2, 4, 2)),
            dma((2, 4, 2)),
            dma((3, 2)),
            dma((2, 4)),
            dma,
            dma,
        ],
        compiler_params=pltpu.CompilerParams(
            collective_id=0, has_side_effects=True, vmem_limit_bytes=VMEM_MIB * 1024 * 1024),
    )(in_hbm(green_recv.reshape(depth_r, points)), in_hbm(green_shot.reshape(depth_s, points)), freq_bins,
      in_hbm(band_mask), in_hbm(live_counts))
    band = pl.pallas_call(
        store_kernel,
        out_shape=jax.ShapeDtypeStruct((slots, half, points), f32),
        in_specs=[pl.BlockSpec(memory_space=pltpu.VMEM)],
        out_specs=anywhere,
        scratch_shapes=[dma((slots,))],
        compiler_params=pltpu.CompilerParams(vmem_limit_bytes=4 * 1024 * 1024),
    )(band)
    return jnp.transpose(band, (1, 0, 2))


def solution(mesh):
    return jax.shard_map(
        per_device,
        mesh=mesh,
        in_specs=(
            P(("grp", "freq"), None, None, "tile"),
            P(("grp", "freq"), None, None, "tile"),
            P("grp", None),
            P("grp"),
            P(("grp", "freq")),
        ),
        out_specs=P(("grp", "tile", "freq"), None, None),
        check_vma=False,
    )
```

time: 59.6 us -> 56.8 us (0.953)
  the two profiles are of different devices: /device:TPU:13 before, /device:TPU:0 now
where the time goes in v1:
time: 56.8 us; the launch traced here: 56.7 us
  Pallas kernels  56 us (99%)
  between operations  0.66 us (1%)
    pallas_call x1, Pallas kernels, per_device(): pl.pallas_call(functools.partial(band_kernel, tiles, slots // 2), out_sha...  54.5 us
    pallas_call x1, Pallas kernels, per_device(): pl.pallas_call(store_kernel, out_shape=jax.ShapeDtypeStruct((slots, half,...  1.53 us

profile of v1, /device:TPU:0, one launch (start us, length us, event | category | flops | bytes accessed | tf_op | source)
XLA Modules:
  0.0 56.7 jit_solution(10455340526284934514)
XLA Ops:
  0.7 54.5 %shard_map.55.band = f32[5,256,512]{2,1,0:T(8,128)S(1)} custom-call(bf16[2048,512]{1,0:T(8,128)(2,1)} %bitcast.3, bf16[1024,512]{1,0:T(8,128)(2,1)} %bitcast.4, s32[1]{0:T(128)S(6)} %copy.6.bins_ref, s32[8,5]{1,0:T(8,128)} %band_hbm.1, s32[8]{0:T(128)} %live_hbm.1), custom_call_target="tpu_custom_call" | custom-call | tf_op jit(solution)/shard_map/pallas_call | solution.py:343
  55.2 1.5 %shard_map.56 = f32[5,256,512]{2,1,0:T(8,128)} custom-call(f32[5,256,512]{2,1,0:T(8,128)S(1)} %shard_map.55.band), custom_call_target="tpu_custom_call" | custom-call | tf_op jit(solution)/shard_map/pallas_call | solution.py:374

commit v2 on v1

--- a/solution.py
+++ b/solution.py
@@ -54,22 +54,25 @@
             device_id={"tile": t - step * distance}, device_id_type=MESH)
 
     barrier = pltpu.get_barrier_semaphore()
-    for distance in range(-2, 3):
-        near = t + distance
-        for turn in range(2):
-            if distance == 0 and turn == 0:
-                continue
-            other = f if turn == 0 else 1 - f
-
-            @pl.when((near >= 0) & (near < tiles))
-            def _():
-                pl.semaphore_signal(barrier, inc=1, device_id={"tile": near, "freq": other}, device_id_type=MESH)
-    reached = jnp.minimum(t, 2) + jnp.minimum(tiles - 1 - t, 2)
+    partner = t + step * jnp.where(heavy, 1, -1)
+
+    def greet(tile, freq):
+        pl.semaphore_signal(barrier, inc=1, device_id={"tile": tile, "freq": freq}, device_id_type=MESH)
+
+    for near in (t - 2, t + 2):
+        @pl.when((near >= 0) & (near < tiles))
+        def _():
+            greet(near, f)
+            greet(near, 1 - f)
+    greet(partner, f)
+    greet(partner, 1 - f)
+    greet(t, 1 - f)
+    greeted = 3 + 2 * ((t >= 2).astype(jnp.int32) + (t + 2 < tiles).astype(jnp.int32))
     for j in range(2):
         for which in range(2):
             own_copy(which, j).start()
 
-    pl.semaphore_wait(barrier, 2 * reached + 1)
+    pl.semaphore_wait(barrier, greeted)
 
     for i in range(4):
         for which in range(2):
@@ -198,21 +201,33 @@
 
     @pl.when(heavy)
     def _():
-        for which in range(2):
-            data_copy(which, 3, 1).wait_recv()
+        data_copy(0, 3, 1).wait_recv()
 
         @pl.loop(0, 6)
         def _(n):
             plain_send(1, n // 2, 0, n % 2, n).start()
 
-        @pl.when(has_far)
-        def _():
-            plain_send(1, 2, 2, 0, 1).start()
-
-            @pl.loop(0, 3)
-            def _(m):
-                turned_send(2, m, 1, 0, 2 * m).start()
-
+    @pl.when(has_far)
+    def _():
+        data_copy(0, 3, 2).wait_recv()
+
+        @pl.loop(0, 6)
+        def _(n):
+            plain_send(2, n // 2, 0, n % 2, n).start()
+
+    @pl.when(heavy & has_far)
+    def _():
+        plain_send(1, 2, 2, 0, 1).start()
+        turned_send(1, 2, 2, 0, 1).start()
+
+        @pl.loop(0, 3)
+        def _(m):
+            plain_send(2, m, 1, 0, 2 * m).start()
+            turned_send(2, m, 1, 0, 2 * m).start()
+
+    @pl.when(heavy)
+    def _():
+        data_copy(1, 3, 1).wait_recv()
         build_left(1, 3)
 
         @pl.loop(0, 2)
@@ -221,21 +236,10 @@
 
     @pl.when(has_far)
     def _():
-        for which in range(2):
-            data_copy(which, 3, 2).wait_recv()
-
-        @pl.loop(0, 6)
-        def _(n):
-            plain_send(2, n // 2, 0, n % 2, n).start()
+        data_copy(1, 3, 2).wait_recv()
 
         @pl.when(heavy)
         def _():
-            turned_send(1, 2, 2, 0, 1).start()
-
-            @pl.loop(0, 3)
-            def _(m):
-                plain_send(2, m, 1, 0, 2 * m).start()
-
             unit(1, 3, 2, 0, 3, True)
 
         build_left(2, 3)

time: 56.8 us -> 52.9 us (0.931)
  the two profiles are of different devices: /device:TPU:0 before, /device:TPU:13 now
where the time goes in v2:
time: 52.9 us; the launch traced here: 52.7 us
  Pallas kernels  52.1 us (98%)
  between operations  0.66 us (1%)
    pallas_call x1, Pallas kernels, per_device(): pl.pallas_call(functools.partial(band_kernel, tiles, slots // 2), out_sha...  50.5 us
    pallas_call x1, Pallas kernels, per_device(): pl.pallas_call(store_kernel, out_shape=jax.ShapeDtypeStruct((slots, half,...  1.53 us

profile of v2, /device:TPU:13, one launch (start us, length us, event | category | flops | bytes accessed | tf_op | source)
XLA Modules:
  0.0 52.7 jit_solution(1750065236755374263)
XLA Ops:
  0.7 50.5 %shard_map.55.band = f32[5,256,512]{2,1,0:T(8,128)S(1)} custom-call(bf16[2048,512]{1,0:T(8,128)(2,1)} %bitcast.3, bf16[1024,512]{1,0:T(8,128)(2,1)} %bitcast.4, s32[1]{0:T(128)S(6)} %copy.6.bins_ref, s32[8,5]{1,0:T(8,128)} %band_hbm.1, s32[8]{0:T(128)} %live_hbm.1), custom_call_target="tpu_custom_call" | custom-call | tf_op jit(solution)/shard_map/pallas_call | solution.py:347
  51.2 1.5 %shard_map.56 = f32[5,256,512]{2,1,0:T(8,128)} custom-call(f32[5,256,512]{2,1,0:T(8,128)S(1)} %shard_map.55.band), custom_call_target="tpu_custom_call" | custom-call | tf_op jit(solution)/shard_map/pallas_call | solution.py:378

commit v3 on v2

--- a/solution.py
+++ b/solution.py
@@ -54,25 +54,19 @@
             device_id={"tile": t - step * distance}, device_id_type=MESH)
 
     barrier = pltpu.get_barrier_semaphore()
-    partner = t + step * jnp.where(heavy, 1, -1)
 
     def greet(tile, freq):
         pl.semaphore_signal(barrier, inc=1, device_id={"tile": tile, "freq": freq}, device_id_type=MESH)
 
-    for near in (t - 2, t + 2):
-        @pl.when((near >= 0) & (near < tiles))
-        def _():
-            greet(near, f)
-            greet(near, 1 - f)
-    greet(partner, f)
-    greet(partner, 1 - f)
+    pl.when(has_far)(lambda: greet(t + 2 * step, f))
+    pl.when(heavy)(lambda: greet(t + step, f))
     greet(t, 1 - f)
-    greeted = 3 + 2 * ((t >= 2).astype(jnp.int32) + (t + 2 < tiles).astype(jnp.int32))
+    greeters = 1 + jnp.where(heavy, 0, 1) + jnp.where(r >= 2, 1, 0)
     for j in range(2):
         for which in range(2):
             own_copy(which, j).start()
 
-    pl.semaphore_wait(barrier, greeted)
+    pl.semaphore_wait(barrier, greeters)
 
     for i in range(4):
         for which in range(2):

time: 52.9 us -> 51.8 us (0.979)
  Pallas kernels: 52.1 us -> 51 us
    pallas_call x1, Pallas kernels: 50.5 us -> 49.5 us  [per_device(): pl.pallas_call(functools.partial(band_kernel, tiles, slots // 2), out_sha...]
where the time goes in v3:
time: 51.8 us; the launch traced here: 51.7 us
  Pallas kernels  51 us (98%)
  between operations  0.66 us (1%)
    pallas_call x1, Pallas kernels, per_device(): pl.pallas_call(functools.partial(band_kernel, tiles, slots // 2), out_sha...  49.5 us
    pallas_call x1, Pallas kernels, per_device(): pl.pallas_call(store_kernel, out_shape=jax.ShapeDtypeStruct((slots, half,...  1.53 us

profile of v3, /device:TPU:13, one launch (start us, length us, event | category | flops | bytes accessed | tf_op | source)
XLA Modules:
  0.0 51.7 jit_solution(788588601460691018)
XLA Ops:
  0.7 49.5 %shard_map.55.band = f32[5,256,512]{2,1,0:T(8,128)S(1)} custom-call(bf16[2048,512]{1,0:T(8,128)(2,1)} %bitcast.3, bf16[1024,512]{1,0:T(8,128)(2,1)} %bitcast.4, s32[1]{0:T(128)S(6)} %copy.6.bins_ref, s32[8,5]{1,0:T(8,128)} %band_hbm.1, s32[8]{0:T(128)} %live_hbm.1), custom_call_target="tpu_custom_call" | custom-call | tf_op jit(solution)/shard_map/pallas_call | solution.py:341
  50.1 1.5 %shard_map.56 = f32[5,256,512]{2,1,0:T(8,128)} custom-call(f32[5,256,512]{2,1,0:T(8,128)S(1)} %shard_map.55.band), custom_call_target="tpu_custom_call" | custom-call | tf_op jit(solution)/shard_map/pallas_call | solution.py:372

commit v4 on v3

--- a/solution.py
+++ b/solution.py
@@ -22,8 +22,8 @@
     return t, f, step, r, lax.rem(r, 2) == 0
 
 
-def band_kernel(tiles, radius, recv_ref, shot_ref, bins_ref, band_hbm, live_hbm, out,
-                band_ref, live_ref, table_sem, inbox, far_r, far_s, left_r, left_s, own, self_out, self_in, outbox, turned,
+def band_kernel(tiles, radius, recv_ref, shot_ref, bins_ref, band_hbm, live_hbm, out, inbox, own,
+                band_ref, live_ref, table_sem, far_r, far_s, left_r, left_s, self_out, self_in, outbox, turned,
                 own_sem, data_send, data_recv, res_send, res_recv, self_send, self_recv):
     t, f, step, r, heavy = place(tiles)
     depth_r, points = recv_ref.shape
@@ -258,40 +258,46 @@
             send_sem=res_send.at[0, 0], recv_sem=res_recv.at[origin, row],
             device_id={"freq": 1 - f}, device_id_type=MESH).wait_recv()
 
+    def kept(delta):
+        near, slot = t + step * delta, radius + step * delta
+        return slot, row_live & (cols < live_ref[near]) & (band_ref[t, slot] > 0)
+
     def emit(delta, value):
-        near, slot = t + step * delta, radius + step * delta
-        keep = row_live & (cols < live_ref[near]) & (band_ref[t, slot] > 0)
+        slot, keep = kept(delta)
         out[slot] = jnp.where(keep, value, 0.0)
+
+    for delta in (1, -1):
+        @pl.when((r + delta >= 0) & (r + delta < tiles))
+        def _():
+            emit(delta, jnp.ones((half, points), jnp.float32))
 
     self_copy().wait_recv()
     emit(0, own[0] + self_in[...])
-    for delta in ROW:
+    for delta in (2, -2):
+        row, mirror = ROW[delta], ROW[-delta]
         exists = (r + delta >= 0) & (r + delta < tiles)
 
+        @pl.when(exists)
+        def _():
+            wait_inbox(1, mirror)
+            if delta == 2:
+                emit(delta, own[delta] + inbox[1, mirror].astype(jnp.float32))
+            else:
+                wait_inbox(0, row)
+                emit(delta, inbox[0, row].astype(jnp.float32) + inbox[1, mirror].astype(jnp.float32))
+
         @pl.when(jnp.logical_not(exists))
         def _():
             out[radius + step * delta] = jnp.zeros((half, points), jnp.float32)
 
-    for delta in (2, -2, 1, -1):
-        row = ROW[delta]
-        exists = (r + delta >= 0) & (r + delta < tiles)
-
-        def own_sum():
+    for delta in (1, -1):
+        @pl.when((r + delta >= 0) & (r + delta < tiles))
+        def _():
             wait_inbox(1, ROW[-delta])
-            emit(delta, own[delta] + inbox[1, ROW[-delta]].astype(jnp.float32))
-
-        def inbox_sum():
-            wait_inbox(0, row)
-            wait_inbox(1, ROW[-delta])
-            emit(delta, inbox[0, row].astype(jnp.float32) + inbox[1, ROW[-delta]].astype(jnp.float32))
-
-        if delta == 2:
-            pl.when(exists)(own_sum)
-        elif delta == 1:
-            pl.when(exists & heavy)(own_sum)
-            pl.when(exists & jnp.logical_not(heavy))(inbox_sum)
-        else:
-            pl.when(exists)(inbox_sum)
+            if delta == 1:
+                pl.when(jnp.logical_not(heavy))(lambda: wait_inbox(0, ROW[delta]))
+            else:
+                wait_inbox(0, ROW[delta])
 
     self_copy().wait_send()
     for i in range(4):
@@ -316,12 +322,39 @@
             wait_sent(turned.at[k] if k == 2 else turned.at[k, 0:4], res_send.at[k, 1])
 
 
-def store_kernel(band, out_ref, out_sem):
-    slots = band.shape[0]
-    for slot in range(slots):
-        pltpu.make_async_copy(band.at[slot], out_ref.at[slot], out_sem.at[slot]).start()
-    for slot in range(slots):
-        pltpu.make_async_copy(band.at[slot], out_ref.at[slot], out_sem.at[slot]).wait()
+def store_kernel(tiles, band, inbox, own, out_ref, late, out_sem):
+    t, f, step, r, heavy = place(tiles)
+    slots, half, points = band.shape
+    radius = slots // 2
+    ready = [slot for slot in range(slots) if abs(slot - radius) != 1]
+    copies = [pltpu.make_async_copy(band.at[slot], out_ref.at[slot], out_sem.at[slot]) for slot in ready]
+    for copy in copies:
+        copy.start()
+    for k, delta in enumerate((1, -1)):
+        slot = radius + step * delta
+        exists = (r + delta >= 0) & (r + delta < tiles)
+
+        def total(first):
+            value = first + inbox[1, ROW[-delta]].astype(jnp.float32)
+            late[k] = jnp.where(band[slot] > 0, value, 0.0)
+
+        def from_inbox():
+            total(inbox[0, ROW[delta]].astype(jnp.float32))
+
+        if delta == 1:
+            pl.when(exists & heavy)(lambda: total(own[1]))
+            pl.when(exists & jnp.logical_not(heavy))(from_inbox)
+        else:
+            pl.when(exists)(from_inbox)
+
+        @pl.when(jnp.logical_not(exists))
+        def _():
+            late[k] = jnp.zeros((half, points), jnp.float32)
+
+        copies.append(pltpu.make_async_copy(late.at[k], out_ref.at[slot], out_sem.at[radius - 1 + 2 * k]))
+        copies[-1].start()
+    for copy in copies:
+        copy.wait()
 
 
 def in_hbm(array):
@@ -338,21 +371,24 @@
     bf16, f32 = jnp.bfloat16, jnp.float32
     dma = pltpu.SemaphoreType.DMA
     anywhere = pl.BlockSpec(memory_space=pltpu.HBM)
-    band = pl.pallas_call(
+    in_vmem = pl.BlockSpec(memory_space=pltpu.VMEM)
+    parts = pl.pallas_call(
         functools.partial(band_kernel, tiles, slots // 2),
-        out_shape=jax.ShapeDtypeStruct((slots, half, points), f32),
+        out_shape=(
+            jax.ShapeDtypeStruct((slots, half, points), f32),
+            jax.ShapeDtypeStruct((2, 4, half, points), bf16),
+            jax.ShapeDtypeStruct((3, half, points), f32),
+        ),
         in_specs=[anywhere, anywhere, pl.BlockSpec(memory_space=pltpu.SMEM), anywhere, anywhere],
-        out_specs=pl.BlockSpec(memory_space=pltpu.VMEM),
+        out_specs=(in_vmem,) * 3,
         scratch_shapes=[
             pltpu.SMEM(band_mask.shape, jnp.int32),
             pltpu.SMEM(live_counts.shape, jnp.int32),
             dma((2,)),
-            pltpu.VMEM((2, 4, half, points), bf16),
             pltpu.VMEM((3, 2, depth_r, half), bf16),
             pltpu.VMEM((3, 2, depth_s, half), bf16),
             pltpu.VMEM((3, 4, half, depth_r), bf16),
             pltpu.VMEM((3, 4, half, depth_s), bf16),
-            pltpu.VMEM((3, half, points), f32),
             pltpu.VMEM((half, points), f32),
             pltpu.VMEM((half, points), f32),
             pltpu.VMEM((3, 8, half // 2, half), bf16),
@@ -370,13 +406,13 @@
     )(in_hbm(green_recv.reshape(depth_r, points)), in_hbm(green_shot.reshape(depth_s, points)), freq_bins,
       in_hbm(band_mask), in_hbm(live_counts))
     band = pl.pallas_call(
-        store_kernel,
+        functools.partial(store_kernel, tiles),
         out_shape=jax.ShapeDtypeStruct((slots, half, points), f32),
-        in_specs=[pl.BlockSpec(memory_space=pltpu.VMEM)],
+        in_specs=[in_vmem] * 3,
         out_specs=anywhere,
-        scratch_shapes=[dma((slots,))],
+        scratch_shapes=[pltpu.VMEM((2, half, points), f32), dma((slots,))],
         compiler_params=pltpu.CompilerParams(vmem_limit_bytes=4 * 1024 * 1024),
-    )(band)
+    )(*parts)
     return jnp.transpose(band, (1, 0, 2))
 
 

time: 51.8 us -> 51.7 us (level)
  no operation moved by 1% of the time
where the time goes in v4:
time: 51.7 us; the launch traced here: 51.5 us
  Pallas kernels  50.9 us (98%)
  between operations  0.66 us (1%)
    pallas_call x1, Pallas kernels, per_device(): pl.pallas_call(functools.partial(band_kernel, tiles, slots // 2), out_sha...  49.4 us
    pallas_call x1, Pallas kernels, per_device(): pl.pallas_call(functools.partial(store_kernel, tiles), out_shape=jax.Shap...  1.53 us

profile of v4, /device:TPU:13, one launch (start us, length us, event | category | flops | bytes accessed | tf_op | source)
XLA Modules:
  0.0 51.5 jit_solution(6885876475550077991)
XLA Ops:
  0.7 49.4 %shard_map.55 = (f32[5,256,512]{2,1,0:T(8,128)S(1)}, bf16[2,4,256,512]{3,2,1,0:T(8,128)(2,1)S(1)}, f32[3,256,512]{2,1,0:T(8,128)S(1)}) custom-call(bf16[2048,512]{1,0:T(8,128)(2,1)} %bitcast.3, bf16[1024,512]{1,0:T(8,128)(2,1)} %bitcast.4, s32[1]{0:T(128)S(6)} %copy.6.bins_ref, s32[8,5]{1,0:T(8,128)} %band_hbm.1, s32[8]{0:T(128)} %live_hbm.1), custom_call_target="tpu_custom_call" | custom-call | tf_op jit(solution)/shard_map/pallas_call | solution.py:375
  50.0 1.5 %shard_map.56 = f32[5,256,512]{2,1,0:T(8,128)} custom-call(f32[5,256,512]{2,1,0:T(8,128)S(1)} %get-tuple-element.8.band, bf16[2,4,256,512]{3,2,1,0:T(8,128)(2,1)S(1)} %get-tuple-element.9.inbox, f32[3,256,512]{2,1,0:T(8,128)S(1)} %get-tuple-element.10.own), custom_call_target="tpu_custom_call" | custom-call | tf_op jit(solution)/shard_map/pallas_call | solution.py:408

commit v5 on v4

--- a/solution.py
+++ b/solution.py
@@ -33,9 +33,6 @@
     has_far = r + 2 < tiles
     tables = [pltpu.make_async_copy(src, dst, table_sem.at[k]) for k, (src, dst) in enumerate(
         ((band_hbm, band_ref), (live_hbm, live_ref)))]
-    for table in tables:
-        table.start()
-
     def columns(j):
         return pl.ds(pl.multiple_of(j * half, half), half)
 
@@ -62,21 +59,24 @@
     pl.when(heavy)(lambda: greet(t + step, f))
     greet(t, 1 - f)
     greeters = 1 + jnp.where(heavy, 0, 1) + jnp.where(r >= 2, 1, 0)
+    pl.semaphore_wait(barrier, greeters)
+
+    for i in range(4):
+        for which in range(2):
+            @pl.when(jnp.logical_not(heavy))
+            def _():
+                data_copy(which, i, 1).start()
+
+            @pl.when(r >= 2)
+            def _():
+                data_copy(which, i, 2).start()
+
+    for table in tables:
+        table.start()
+
     for j in range(2):
         for which in range(2):
             own_copy(which, j).start()
-
-    pl.semaphore_wait(barrier, greeters)
-
-    for i in range(4):
-        for which in range(2):
-            @pl.when(jnp.logical_not(heavy))
-            def _():
-                data_copy(which, i, 1).start()
-
-            @pl.when(r >= 2)
-            def _():
-                data_copy(which, i, 2).start()
 
     def build_left(slot, i):
         for src, dst, depth in ((far_r, left_r, depth_r // 2), (far_s, left_s, depth_s // 2)):
@@ -205,9 +205,12 @@
     def _():
         data_copy(0, 3, 2).wait_recv()
 
-        @pl.loop(0, 6)
-        def _(n):
-            plain_send(2, n // 2, 0, n % 2, n).start()
+        def release():
+            @pl.loop(0, 6)
+            def _(n):
+                plain_send(2, n // 2, 0, n % 2, n).start()
+
+        pl.when(heavy)(release)
 
     @pl.when(heavy & has_far)
     def _():
@@ -231,6 +234,12 @@
     @pl.when(has_far)
     def _():
         data_copy(1, 3, 2).wait_recv()
+
+        @pl.when(jnp.logical_not(heavy))
+        def _():
+            @pl.loop(0, 6)
+            def _(n):
+                plain_send(2, n // 2, 0, n % 2, n).start()
 
         @pl.when(heavy)
         def _():

time: 51.7 us -> 51.7 us (level)
  no operation moved by 1% of the time
where the time goes in v5:
time: 51.7 us; the launch traced here: 51.5 us
  Pallas kernels  50.9 us (98%)
  between operations  0.66 us (1%)
    pallas_call x1, Pallas kernels, per_device(): pl.pallas_call(functools.partial(band_kernel, tiles, slots // 2), out_sha...  49.4 us
    pallas_call x1, Pallas kernels, per_device(): pl.pallas_call(functools.partial(store_kernel, tiles), out_shape=jax.Shap...  1.53 us

profile of v5, /device:TPU:13, one launch (start us, length us, event | category | flops | bytes accessed | tf_op | source)
XLA Modules:
  0.0 51.5 jit_solution(14646159494232578699)
XLA Ops:
  0.7 49.4 %shard_map.55 = (f32[5,256,512]{2,1,0:T(8,128)S(1)}, bf16[2,4,256,512]{3,2,1,0:T(8,128)(2,1)S(1)}, f32[3,256,512]{2,1,0:T(8,128)S(1)}) custom-call(bf16[2048,512]{1,0:T(8,128)(2,1)} %bitcast.3, bf16[1024,512]{1,0:T(8,128)(2,1)} %bitcast.4, s32[1]{0:T(128)S(6)} %copy.6.bins_ref, s32[8,5]{1,0:T(8,128)} %band_hbm.1, s32[8]{0:T(128)} %live_hbm.1), custom_call_target="tpu_custom_call" | custom-call | tf_op jit(solution)/shard_map/pallas_call | solution.py:384
  50.0 1.5 %shard_map.56 = f32[5,256,512]{2,1,0:T(8,128)} custom-call(f32[5,256,512]{2,1,0:T(8,128)S(1)} %get-tuple-element.8.band, bf16[2,4,256,512]{3,2,1,0:T(8,128)(2,1)S(1)} %get-tuple-element.9.inbox, f32[3,256,512]{2,1,0:T(8,128)S(1)} %get-tuple-element.10.own), custom_call_target="tpu_custom_call" | custom-call | tf_op jit(solution)/shard_map/pallas_call | solution.py:417

commit v6 on v4

--- a/solution.py
+++ b/solution.py
@@ -273,6 +273,17 @@
 
     self_copy().wait_recv()
     emit(0, own[0] + self_in[...])
+    self_copy().wait_send()
+    for i in range(4):
+        for which in range(2):
+            @pl.when(jnp.logical_not(heavy))
+            def _():
+                data_copy(which, i, 1).wait_send()
+
+            @pl.when(r >= 2)
+            def _():
+                data_copy(which, i, 2).wait_send()
+
     for delta in (2, -2):
         row, mirror = ROW[delta], ROW[-delta]
         exists = (r + delta >= 0) & (r + delta < tiles)
@@ -298,17 +309,6 @@
                 pl.when(jnp.logical_not(heavy))(lambda: wait_inbox(0, ROW[delta]))
             else:
                 wait_inbox(0, ROW[delta])
-
-    self_copy().wait_send()
-    for i in range(4):
-        for which in range(2):
-            @pl.when(jnp.logical_not(heavy))
-            def _():
-                data_copy(which, i, 1).wait_send()
-
-            @pl.when(r >= 2)
-            def _():
-                data_copy(which, i, 2).wait_send()
 
     def wait_sent(box, sem):
         pltpu.make_async_remote_copy(

time: 51.7 us -> 51.7 us (level)
  no operation moved by 1% of the time
where the time goes in v6:
time: 51.7 us; the launch traced here: 51.5 us
  Pallas kernels  50.9 us (98%)
  between operations  0.66 us (1%)
    pallas_call x1, Pallas kernels, per_device(): pl.pallas_call(functools.partial(band_kernel, tiles, slots // 2), out_sha...  49.3 us
    pallas_call x1, Pallas kernels, per_device(): pl.pallas_call(functools.partial(store_kernel, tiles), out_shape=jax.Shap...  1.53 us

profile of v6, /device:TPU:13, one launch (start us, length us, event | category | flops | bytes accessed | tf_op | source)
XLA Modules:
  0.0 51.5 jit_solution(1041317737086606450)
XLA Ops:
  0.7 49.3 %shard_map.55 = (f32[5,256,512]{2,1,0:T(8,128)S(1)}, bf16[2,4,256,512]{3,2,1,0:T(8,128)(2,1)S(1)}, f32[3,256,512]{2,1,0:T(8,128)S(1)}) custom-call(bf16[2048,512]{1,0:T(8,128)(2,1)} %bitcast.3, bf16[1024,512]{1,0:T(8,128)(2,1)} %bitcast.4, s32[1]{0:T(128)S(6)} %copy.6.bins_ref, s32[8,5]{1,0:T(8,128)} %band_hbm.1, s32[8]{0:T(128)} %live_hbm.1), custom_call_target="tpu_custom_call" | custom-call | tf_op jit(solution)/shard_map/pallas_call | solution.py:375
  50.0 1.5 %shard_map.56 = f32[5,256,512]{2,1,0:T(8,128)} custom-call(f32[5,256,512]{2,1,0:T(8,128)S(1)} %get-tuple-element.8.band, bf16[2,4,256,512]{3,2,1,0:T(8,128)(2,1)S(1)} %get-tuple-element.9.inbox, f32[3,256,512]{2,1,0:T(8,128)S(1)} %get-tuple-element.10.own), custom_call_target="tpu_custom_call" | custom-call | tf_op jit(solution)/shard_map/pallas_call | solution.py:408
